TPU v7x, 32 devices: a whole 2x2x4 slice. The times are simulated.
32 devices in a mesh: seq: 8 (over z, x), batch: 4 (over y, core).
Axes of the slice: x: 2, y: 2, z: 4, core: 2. Of those that a mesh axis runs over, the one named last changes fastest.
Arguments:
- inputs: float32 [4, 1024, 768], P('batch', 'seq'), may hold values from -6 to 6
- norm_gain: float32 [768], replicated, may hold values from 0.5 to 1.5
- input_projection_weight: float32 [768, 3072], replicated, may hold values from -0.21875 to 0.21875
- conv_weight: float32 [4, 1536], replicated, may hold values from -3 to 3
- conv_bias: float32 [1536], replicated, may hold values from -3 to 3
- x_proj: float32 [1536, 80], replicated, may hold values from -0.15625 to 0.15625
- step_proj: float32 [48, 1536], replicated, may hold values from -0.875 to 0.875
- step_bias: float32 [1536], replicated, may hold values from -3 to -1
- decay_code: int32 [1536], replicated, may hold values from 0 to 9
- decay_log: float32 [1536, 16], replicated, may hold values from -5 to -1.5
- skip_gain: float32 [1536], replicated, may hold values from 0.5 to 1.5
- output_projection_weight: float32 [1536, 768], replicated, may hold values from -0.15625 to 0.15625
- cotangent: float32 [4, 1024, 768], P('batch', 'seq'), may hold values from -6 to 6
Outputs:
- block_out: float32 [4, 1024, 768], P('batch', 'seq')
- input_grad: float32 [4, 1024, 768], P('batch', 'seq')
- norm_gain_grad: float32 [768], replicated
- in_proj_grad: float32 [768, 3072], replicated
- conv_weight_grad: float32 [4, 1536], replicated
- conv_bias_grad: float32 [1536], replicated
- x_proj_grad: float32 [1536, 80], replicated
- step_proj_grad: float32 [48, 1536], replicated
- step_bias_grad: float32 [1536], replicated
- decay_log_grad: float32 [1536, 16], replicated
- skip_gain_grad: float32 [1536], replicated
- out_proj_grad: float32 [1536, 768], replicated
All inputs are finite; a program needn't handle non-finite values.
Results may differ from a plain program's by a relative error of at most 0.0003.
Values sent between devices are 32-bit elements; how exact they have to be, the bound alone decides.
A program may use at most 128 MiB of HBM per device.

v0:
```python
from functools import partial
import jax
import jax.numpy as jnp
from jax import lax
from jax.sharding import PartitionSpec as P

QB = 32
MATMUL_ACCURACY = lax.Precision.HIGHEST
EPSILON = 1e-05


def shifted(x, axis, by):
    length = lax.axis_size(axis)
    pairs = [(i, i + by) for i in range(length) if 0 <= i + by < length]
    return lax.ppermute(x, axis, pairs)


def prefix(value, axis, join, neutral, backward):
    count, mine = (lax.axis_size(axis), lax.axis_index(axis))
    pieces = jax.tree.map(lambda part: lax.all_gather(part, axis), value)
    if backward:
        pieces = jax.tree.map(lambda part: part[::-1], pieces)
        mine = count - 1 - mine
    subtotal = jax.tree.map(
        lambda part, zero: jnp.full_like(part, 0) + jnp.asarray(zero, part.dtype), value, neutral
    )

    def turn(position, subtotal):
        longer = join(subtotal, jax.tree.map(lambda part: part[position], pieces))
        return jax.tree.map(lambda new, old: jnp.where(position < mine, new, old), longer, subtotal)

    return lax.fori_loop(0, count - 1, turn, subtotal)


def matmul(left, right):
    return jnp.dot(left, right, precision=MATMUL_ACCURACY, preferred_element_type=jnp.float32)


def silu_grad(value):
    sigma = jax.nn.sigmoid(value)
    return sigma * (1.0 + value * (1.0 - sigma))


def pair_combine(first, second):
    return (first[0] * second[0], first[1] * second[0] + second[1])


def block_states(factor, source, start):
    cumulative_decay_factor, cum_source = lax.associative_scan(
        pair_combine, (factor, source), axis=0
    )
    return cum_source + cumulative_decay_factor * start[None]


def join_carry(negative_decay_rate, earlier, later):
    return (
        earlier[0] + later[0],
        earlier[1] * jnp.exp(negative_decay_rate[None] * later[0][:, None, :]) + later[1],
    )


def adjoint(factor, values, carry):
    alpha = jnp.concatenate([factor[1:], jnp.ones_like(factor[:1])], axis=0)
    return block_states(alpha[::-1], values[::-1], carry)[::-1]


def shards(
    inputs,
    norm_gain,
    input_projection_weight,
    conv_weight,
    conv_bias,
    x_proj,
    step_proj,
    step_bias,
    decay_code,
    decay_log,
    skip_gain,
    output_projection_weight,
    cotangent,
):
    seqs, group, width = inputs.shape
    inner = input_projection_weight.shape[1] // 2
    rank = step_proj.shape[0]
    states = decay_log.shape[1]
    taps = conv_weight.shape[0]
    blocks = group // QB
    rows = seqs * group

    def to_blocks(value):
        cols = value.shape[-1]
        return jnp.swapaxes(value.reshape(seqs, group, cols), 0, 1).reshape(blocks, QB, seqs, cols)

    def from_blocks(value):
        cols = value.shape[-1]
        return jnp.swapaxes(value.reshape(group, seqs, cols), 0, 1).reshape(rows, cols)

    def unpack(packed_blk):
        step_blk = packed_blk[..., :inner]
        mixed_blk = packed_blk[..., inner : 2 * inner]
        b_blk = packed_blk[..., 2 * inner : 2 * inner + states]
        c_blk = packed_blk[..., 2 * inner + states :]
        return (step_blk, mixed_blk, b_blk, c_blk)

    flat_in = inputs.reshape(rows, width)
    rms = lax.rsqrt(jnp.mean(flat_in * flat_in, axis=1, keepdims=True) + EPSILON)
    normalized_input = flat_in * rms * norm_gain
    mixer_and_gate = matmul(normalized_input, input_projection_weight)
    hidden_x = mixer_and_gate[:, :inner].reshape(seqs, group, inner)
    gate_z = mixer_and_gate[:, inner:]
    rim = shifted(hidden_x[:, group - taps + 1 :], "seq", 1)
    padded = jnp.concatenate([rim, hidden_x], axis=1)
    conv = conv_bias + conv_weight[0] * padded[:, 0:group]
    for k in range(1, taps):
        conv = conv + conv_weight[k] * padded[:, k : k + group]
    conv = conv.reshape(rows, inner)
    mixed = jax.nn.silu(conv)
    proj = matmul(mixed, x_proj)
    low_rank = proj[:, :rank]
    pre = matmul(low_rank, step_proj) + step_bias - 0.5 * decay_code.astype(jnp.float32)
    step = jax.nn.softplus(pre)
    negative_decay_rate = -jnp.exp(decay_log).T
    packed_blocks = to_blocks(jnp.concatenate([step, mixed, proj[:, rank:]], axis=1))
    zero_state = jnp.zeros((seqs, states, inner), jnp.float32)
    zero_sum = jnp.zeros((seqs, inner), jnp.float32)

    def terms(step_blk, mixed_blk, b_blk):
        factor = jnp.exp(step_blk[:, :, None, :] * negative_decay_rate)
        source = (step_blk * mixed_blk)[:, :, None, :] * b_blk[:, :, :, None]
        return (factor, source)

    def local_block(state, packed_blk):
        step_blk, mixed_blk, b_blk, c_blk = unpack(packed_blk)
        factor, source = terms(step_blk, mixed_blk, b_blk)
        held = block_states(factor, source, state)
        output = jnp.sum(held * c_blk[:, :, :, None], axis=2)
        return (held[-1], (output, state))

    end_state, (local_out, local_starts) = lax.scan(local_block, zero_state, packed_blocks)
    group_sum = jnp.sum(step.reshape(seqs, group, inner), axis=1)
    combine = partial(join_carry, negative_decay_rate)
    identity = (jnp.zeros_like(group_sum), zero_state)
    start_state = prefix((group_sum, end_state), "seq", combine, identity, False)[1]

    def shift_in(total, data):
        packed_blk, out_blk = data
        step_blk, mixed_blk, b_blk, c_blk = unpack(packed_blk)
        inside = total[None] + jnp.cumsum(step_blk, axis=0)
        decay = jnp.exp(inside[:, :, None, :] * negative_decay_rate)
        output = out_blk + jnp.sum(decay * start_state[None] * c_blk[:, :, :, None], axis=2)
        begin = jnp.exp(total[:, None, :] * negative_decay_rate) * start_state
        return (inside[-1], (output, begin))

    _, (scanned, begins) = lax.scan(shift_in, zero_sum, (packed_blocks, local_out))
    starts = local_starts + begins
    result = from_blocks(scanned) + skip_gain * mixed
    gate_act = jax.nn.silu(gate_z)
    gate_applied_output = result * gate_act
    block_out = (flat_in + matmul(gate_applied_output, output_projection_weight)).reshape(
        seqs, group, width
    )
    flat_cot = cotangent.reshape(rows, width)
    d_gated = matmul(flat_cot, output_projection_weight.T)
    out_grad = matmul(gate_applied_output.T, flat_cot)
    d_result = d_gated * gate_act
    d_gate = d_gated * result * silu_grad(gate_z)
    skip_grad = jnp.sum(d_result * mixed, axis=0)
    dres_blocks = to_blocks(d_result)

    def collect_back(acc, data):
        total, lam_in = acc
        packed_blk, dres_blk = data
        step_blk, mixed_blk, b_blk, c_blk = unpack(packed_blk)
        inside = total[None] + jnp.cumsum(step_blk, axis=0)
        decay = jnp.exp(inside[:, :, None, :] * negative_decay_rate)
        lam_in = lam_in + jnp.sum(decay * c_blk[:, :, :, None] * dres_blk[:, :, None, :], axis=0)
        return ((inside[-1], lam_in), None)

    (_, later_in), _ = lax.scan(collect_back, (zero_sum, zero_state), (packed_blocks, dres_blocks))
    after_state = prefix((group_sum, later_in), "seq", combine, identity, True)[1]

    def full_back(carry, data):
        lam_next, rate_acc = carry
        packed_blk, dres_blk, start = data
        step_blk, mixed_blk, b_blk, c_blk = unpack(packed_blk)
        factor, source = terms(step_blk, mixed_blk, b_blk)
        held = block_states(factor, source, start)
        prior = jnp.concatenate([start[None], held[:-1]], axis=0)
        lam = adjoint(factor, c_blk[:, :, :, None] * dres_blk[:, :, None, :], lam_next)
        c_grad = jnp.sum(held * dres_blk[:, :, None, :], axis=3)
        decayed = lam * prior * factor
        lam_b = jnp.sum(lam * b_blk[:, :, :, None], axis=2)
        step_grad = jnp.sum(decayed * negative_decay_rate, axis=2) + mixed_blk * lam_b
        rate_acc = rate_acc + jnp.sum(decayed * step_blk[:, :, None, :], axis=(0, 1))
        mixed_scan = step_blk * lam_b
        b_grad = jnp.sum(lam * (step_blk * mixed_blk)[:, :, None, :], axis=3)
        joined = jnp.concatenate([step_grad, mixed_scan, b_grad, c_grad], axis=-1)
        return ((factor[0] * lam[0], rate_acc), joined)

    rate_zero = jnp.zeros((states, inner), jnp.float32)
    (_, rate_sum), back_blocks = lax.scan(
        full_back, (after_state, rate_zero), (packed_blocks, dres_blocks, starts), reverse=True
    )
    back_rows = from_blocks(back_blocks)
    step_grad = back_rows[:, :inner]
    mixed_scan = back_rows[:, inner : 2 * inner]
    b_grad = back_rows[:, 2 * inner : 2 * inner + states]
    c_grad = back_rows[:, 2 * inner + states :]
    decay_grad = (rate_sum * negative_decay_rate).T
    pre_grad = step_grad * jax.nn.sigmoid(pre)
    bias_grad = jnp.sum(pre_grad, axis=0)
    step_proj_grad = matmul(low_rank.T, pre_grad)
    proj_grad = jnp.concatenate([matmul(pre_grad, step_proj.T), b_grad, c_grad], axis=1)
    x_proj_grad = matmul(mixed.T, proj_grad)
    mixed_grad = mixed_scan + d_result * skip_gain + matmul(proj_grad, x_proj.T)
    conv_grad = (mixed_grad * silu_grad(conv)).reshape(seqs, group, inner)
    tap_grads = jnp.stack(
        [jnp.sum(conv_grad * padded[:, k : k + group], axis=(0, 1)) for k in range(taps)]
    )
    conv_bias_grad = jnp.sum(conv_grad, axis=(0, 1))
    spread = jnp.zeros((seqs, group + taps - 1, inner), jnp.float32)
    for k in range(taps):
        spread = spread.at[:, k : k + group].add(conv_weight[k] * conv_grad)
    back_rim = shifted(spread[:, : taps - 1], "seq", -1)
    x_grad = spread[:, taps - 1 :].at[:, group - taps + 1 :].add(back_rim)
    both_grad = jnp.concatenate([x_grad.reshape(rows, inner), d_gate], axis=1)
    in_grad = matmul(normalized_input.T, both_grad)
    normed_grad = matmul(both_grad, input_projection_weight.T)
    gain_grad = jnp.sum(normed_grad * flat_in * rms, axis=0)
    weighted = normed_grad * norm_gain
    input_grad = (
        rms * weighted
        - rms * rms * rms * flat_in * jnp.mean(weighted * flat_in, axis=1, keepdims=True)
        + flat_cot
    )
    input_grad = input_grad.reshape(seqs, group, width)
    summed_all = lax.psum(
        (
            gain_grad,
            in_grad,
            tap_grads,
            conv_bias_grad,
            x_proj_grad,
            step_proj_grad,
            bias_grad,
            decay_grad,
            skip_grad,
            out_grad,
        ),
        ("seq", "batch"),
    )
    summed = summed_all[:8]
    skip_sum = summed_all[8]
    out_sum = summed_all[9]
    return (
        block_out,
        input_grad,
        summed[0],
        summed[1],
        summed[2],
        summed[3],
        summed[4],
        summed[5],
        summed[6],
        summed[7],
        skip_sum,
        out_sum,
    )


def solution(mesh):
    return jax.shard_map(
        shards,
        mesh=mesh,
        in_specs=(
            P("batch", "seq", None),
            P(),
            P(),
            P(),
            P(),
            P(),
            P(),
            P(),
            P(),
            P(),
            P(),
            P(),
            P("batch", "seq", None),
        ),
        out_specs=(
            P("batch", "seq", None),
            P("batch", "seq", None),
            P(),
            P(),
            P(),
            P(),
            P(),
            P(),
            P(),
            P(),
            P(),
            P(),
        ),
        check_vma=False,
    )
```

profile of v0, /device:TPU:0, one launch (start us, length us, event | category | flops | bytes accessed | tf_op | source)
XLA Modules:
  0.0 2101.1 jit_solution(8007326374587562995)
XLA Ops:
  9.0 7.8 fusion.71
  23.4 10.2 multiply_reduce_fusion.8
  37.9 33.2 %all-gather.3 = f32[8,1,1536]{2,1,0:T(1,128)S(1)} all-gather(f32[1,1,1536]{2,1,0:T(1,128)S(1)} %reshape.758), channel_id=2, replica_groups=mesh['seq'=8,'batch'=4] {'seq'}, dimensions={0}, use_global_device_ids=true | all-gather | bytes 55296 | tf_op jit(solution)/shard_map/all_gather | solution.py:20
  75.0 414.5 %while.93 = (s32[]{:T(128)}, f32[1,16,1536]{2,1,0:T(8,128)}, f32[4,32,1,1536]{3,2,1,0:T(1,128)}, f32[4,1,16,1536]{3,2,1,0:T(8,128)}, f32[4,32,1,3104]{3,2,1,0:T(...) while((s32[]{:T(128)}, f32[1,16,1536]{2,1,0:T(8,128)}, f32[4,32,1,1536]{3,2,1,0:T(1,128)}, ...), condition=%wide.region_3.4_spmd, body=%wide.region_1.3_spmd.sunk | while | flops 14721026 | bytes 223114064 | solution.py:139
  134.8 10.9 pad.889
  145.7 6.8 pad.887
  152.6 10.9 pad.890
  163.5 6.8 pad.888
  238.4 10.9 pad.889
  249.3 6.8 pad.887
  256.2 10.9 pad.890
  267.1 6.8 pad.888
  342.1 10.9 pad.889
  353.0 6.8 pad.887
  359.8 10.9 pad.890
  370.8 6.8 pad.888
  445.7 10.9 pad.889
  456.6 6.8 pad.887
  463.4 10.9 pad.890
  474.4 6.8 pad.888
  489.5 10.9 while.96
  500.4 32.3 %all-gather.2 = f32[8,16,1536]{2,1,0:T(8,128)S(1)} all-gather(f32[1,16,1536]{2,1,0:T(8,128)} %get-tuple-element.564), channel_id=4, replica_groups=mesh['seq'=8,'batch'=4] {'seq'}, dimensions={0}, use_global_device_ids=true | all-gather | bytes 884736 | tf_op jit(solution)/shard_map/all_gather | solution.py:20
  533.7 11.9 while.97
  545.6 34.0 %all-gather.1 = f32[8,16,1536]{2,1,0:T(8,128)} all-gather(f32[1,16,1536]{2,1,0:T(8,128)} %get-tuple-element.561), channel_id=3, replica_groups=mesh['seq'=8,'batch'=4] {'seq'}, dimensions={0}, use_global_device_ids=true | all-gather | bytes 884736 | tf_op jit(solution)/shard_map/all_gather | solution.py:20
  579.6 11.9 while.95
  591.6 12.4 while.94
  607.0 883.2 %while.98 = (s32[]{:T(128)}, f32[1,16,1536]{2,1,0:T(8,128)S(1)}, f32[16,1536]{1,0:T(8,128)}, f32[4,32,1,3104]{3,1,2,0:T(8,128)}, f32[4,32,1,3104]{3,2,1,0:T(1,12...) while((s32[]{:T(128)}, f32[1,16,1536]{2,1,0:T(8,128)S(1)}, ...), condition=%wide.region_23.24_spmd.clone, body=%wide.region_17.23_spmd.clone.sunk | while | flops 36273152 | bytes 493608896 | solution.py:201
  675.3 10.9 pad.945
  686.3 6.8 pad.943
  693.1 10.9 pad.946
  704.0 7.0 pad.944
  778.4 10.9 pad.961
  789.4 6.8 pad.959
  796.2 11.1 pad.962
  807.3 6.8 pad.960
  896.0 10.9 pad.945
  906.9 6.8 pad.943
  913.8 10.9 pad.946
  924.7 7.0 pad.944
  999.1 10.9 pad.961
  1010.0 6.8 pad.959
  1016.9 11.1 pad.962
  1027.9 6.8 pad.960
  1116.6 10.9 pad.945
  1127.5 6.8 pad.943
  1134.4 10.9 pad.946
  1145.3 7.0 pad.944
  1219.7 10.9 pad.961
  1230.7 6.8 pad.959
  1237.5 11.1 pad.962
  1248.6 6.8 pad.960
  1337.3 10.9 pad.945
  1348.2 6.8 pad.943
  1355.1 10.9 pad.946
  1366.0 7.0 pad.944
  1440.4 10.9 pad.961
  1458.2 11.1 pad.962
  1469.2 6.8 pad.960
  1515.0 7.3 fusion.58
  1526.4 11.3 fusion.44
  1544.0 12.2 fusion.69
  1556.2 43.1 %all-reduce.63 = (f32[768]{0:T(1024)}, f32[4,1536]{1,0:T(4,128)}, f32[1536]{0:T(1024)}, f32[1536]{0:T(1024)}, f32[1536]{0:T(1024)}) all-reduce(f32[768]{0:T(1024)S(1)} %get-tuple-element.805, f32[4,1536]{1,0:T(4,128)S(1)} %pad_maximum_fusion.31, ...), channel_id=1, replica_groups=mesh['seq'=8,'batch'=4] {'seq','batch'}, use_global_device_ids=true, to_apply=%region_26.27 | all-reduce | flops 11520 | bytes 92160 | tf_op jit(solution)/shard_map/psum | solution.py:237
  1600.3 480.7 %all-reduce.67.cloned.1.call-done = (f32[768,3072]{1,0:T(8,128)}, f32[1536,80]{0,1:T(8,128)}, f32[48,1536]{1,0:T(8,128)}, f32[1536,16]{0,1:T(8,128)}, f32[1536,768]{1,0:T(8,128)}) async-done(((f32[768,3072]{1,0:T(8,128)}, f32[1536,80]{0,1:T(8,128)}, f32[48,1536]{1,0:T(8,128)}, f32[1536,16]{0,1:T(8,128)}, f32[1536,768]{1,0:T(8,128)}), (f32[768,3072]{1,0:T(8,128)}, f32[1536,80]{0,1:T(8,128)}, ...) | async-done | bytes 15040528 | tf_op jit(solution)/shard_map/psum | solution.py:237
  2081.0 8.8 copy.196
  (1577 shorter events, 978.9 us)
Async XLA Ops:
  7.2 26.5 %copy-start = (f32[1536,80]{0,1:T(8,128)S(1)}, f32[1536,80]{0,1:T(8,128)}, u32[]{:S(2)}) copy-start(f32[1536,80]{0,1:T(8,128)} %param.40) | copy-start | bytes 1474564
  7.2 2073.8 %all-reduce.67.cloned.1.call-start = ((), (), s32[]{:S(2)}) async-start(), calls=%async_computation | async-start | bytes 30081024 | tf_op jit(solution)/shard_map/psum | solution.py:237
  9.0 7.8 copy-start.125
  16.8 16.9 copy-start.60
  16.8 6.6 copy-start.100
  16.9 6.5 collective-permute-start
  22.1 11.6 copy-start.114
  22.1 11.6 copy-start.116
  22.1 11.6 copy-start.118
  22.1 11.6 copy-start.120
  23.4 10.3 copy-start.122
  23.4 11.3 copy-start.132
  33.7 38.0 %copy-start.63 = (f32[128,1536]{1,0:T(8,128)}, f32[128,1536]{1,0:T(8,128)S(1)}, u32[]{:S(2)}) copy-start(f32[128,1536]{1,0:T(8,128)S(1)} %get-tuple-element.907) | copy-start | bytes 2359300
  152.6 10.9 copy-start.29
  170.4 8.2 copy-start.52
  256.2 10.9 copy-start.29
  274.0 8.3 copy-start.52
  359.8 10.9 copy-start.29
  377.6 8.2 copy-start.52
  463.4 10.9 copy-start.29
  481.2 8.2 copy-start.52
  500.4 33.3 %copy-start.69 = (f32[1,16,1536]{2,1,0:T(8,128)S(1)}, f32[1,16,1536]{2,1,0:T(8,128)}, u32[]{:S(2)}) copy-start(f32[1,16,1536]{2,1,0:T(8,128)} %custom-call.2) | copy-start | bytes 294916
  533.7 46.0 %copy-start.87 = (f32[1,16,1536]{2,1,0:T(8,128)S(1)}, f32[1,16,1536]{2,1,0:T(8,128)}, u32[]{:S(2)}) copy-start(f32[1,16,1536]{2,1,0:T(8,128)} %custom-call) | copy-start | bytes 294916
  607.2 7.7 copy-start.36
  693.1 10.9 copy-start.31
  704.0 7.0 copy-start.71
  711.1 7.0 copy-start.57
  796.2 11.1 copy-start.30
  807.3 6.9 copy-start.56
  807.3 6.9 copy-start.68
  827.9 7.7 copy-start.36
  913.8 10.9 copy-start.31
  924.7 7.0 copy-start.71
  931.7 7.0 copy-start.57
  1016.9 11.1 copy-start.30
  1027.9 6.9 copy-start.56
  1027.9 6.9 copy-start.68
  1048.5 7.7 copy-start.36
  1134.4 10.9 copy-start.31
  1145.3 7.0 copy-start.71
  1152.4 7.0 copy-start.57
  1237.5 11.1 copy-start.30
  1248.6 6.9 copy-start.56
  1248.6 6.9 copy-start.68
  1269.2 7.7 copy-start.36
  1355.1 10.9 copy-start.31
  1366.0 7.0 copy-start.71
  1373.0 7.0 copy-start.57
  1458.2 11.1 copy-start.30
  1469.2 6.9 copy-start.56
  1469.2 6.9 copy-start.68
  1507.5 7.5 copy-start.101
  1513.6 11.1 collective-permute-start.1
  1514.9 7.4 copy-start.90
  1514.9 7.4 copy-start.99
  1515.0 7.4 copy-start.115
  1515.0 7.4 copy-start.123
  1544.0 12.3 copy-start.129
  1544.0 55.4 %copy-start.102 = (f32[1,128,768]{2,1,0:T(8,128)S(1)}, f32[1,128,768]{2,1,0:T(8,128)}, u32[]{:S(2)}) copy-start(f32[1,128,768]{2,1,0:T(8,128)} %param.47) | copy-start | bytes 1179652
  1544.0 55.4 %copy-start.130 = (f32[128]{0:T(128)S(1)}, f32[128]{0:T(128)}, u32[]{:S(2)}) copy-start(f32[128]{0:T(128)} %get-tuple-element.1005) | copy-start | bytes 1540
  2081.0 10.9 slice-start.1
  2081.0 8.8 copy-start.105
  2081.0 9.5 copy-start.108
  2081.0 10.9 slice-start.2
  (324 other events, 773.8 us)
Sparse Core Ops, SparseCore 0:
  1537.8 543.1 all-reduce.66
where the time goes:
time: 2130 us; the launch traced here: 2100 us
  local copies, waits for them, and re-layouts  1010 us (47%)
  waiting for transfers between devices  482 us (23%)
  other arithmetic  379 us (18%)
  blocking collectives  143 us (7%)
  matrix products  65.5 us (3%)
    pad x192, local copies, waits for them, and re-layouts, block_states(): lax.associative_scan(pair_combine, (factor, source), axis=0)  811 us
    psum x1, waiting for transfers between devices, shards(): lax.psum((gain_grad, in_grad, tap_grads, conv_bias_grad, x_proj_grad, ste...  481 us
    add x96, other arithmetic, pair_combine(): return (first[0] * second[0], first[1] * second[0] + second[1])  105 us
    all_gather x3, blocking collectives, prefix(): pieces = jax.tree.map(lambda part: lax.all_gather(part, axis), value)  99.6 us
    add x96, other arithmetic, block_states(): lax.associative_scan(pair_combine, (factor, source), axis=0)  87.8 us
    dot_general x12, matrix products, matmul(): jnp.dot(left, right, precision=MATMUL_ACCURACY, preferred_element_type=jn...  65.5 us
    slice x84, local copies, waits for them, and re-layouts, block_states(): lax.associative_scan(pair_combine, (factor, source), axis=0)  54.1 us
    while x668, local copies, waits for them, and re-layouts  49 us
  transfers between devices with their start and end apart: 3, of which 2 were waited for; matrix products, arithmetic and copies ran while one was open for 1% of the time, Pallas kernels for 0%

commit v1 on v0

--- a/solution.py
+++ b/solution.py
@@ -235,19 +235,22 @@
     )
     input_grad = input_grad.reshape(seqs, group, width)
     summed_all = lax.psum(
-        (
-            gain_grad,
-            in_grad,
-            tap_grads,
-            conv_bias_grad,
-            x_proj_grad,
-            step_proj_grad,
-            bias_grad,
-            decay_grad,
-            skip_grad,
-            out_grad,
+        lax.psum(
+            (
+                gain_grad,
+                in_grad,
+                tap_grads,
+                conv_bias_grad,
+                x_proj_grad,
+                step_proj_grad,
+                bias_grad,
+                decay_grad,
+                skip_grad,
+                out_grad,
+            ),
+            "batch",
         ),
-        ("seq", "batch"),
+        "seq",
     )
     summed = summed_all[:8]
     skip_sum = summed_all[8]

time: 2130 us -> 2320 us (1.089)
  waiting for transfers between devices: 482 us -> 665 us
    psum x0 -> x1, waiting for transfers between devices: none -> 401 us  [shards(): lax.psum(lax.psum((gain_grad, in_grad, tap_grads, conv_bias_grad, x_proj_...]
    psum x1, waiting for transfers between devices: 481 us -> 263 us  [shards(): lax.psum((gain_grad, in_grad, tap_grads, conv_bias_grad, x_proj_grad, ste...]
    psum x0 -> x1, blocking collectives: none -> 41.8 us  [shards(): lax.psum(lax.psum((gain_grad, in_grad, tap_grads, conv_bias_grad, x_proj_...]
    psum x1, blocking collectives: 43.1 us -> 11.5 us  [shards(): lax.psum((gain_grad, in_grad, tap_grads, conv_bias_grad, x_proj_grad, ste...]
  transfers between devices with their start and end apart: 3 -> 4, of which waited for: 2 -> 3; matrix products, arithmetic and copies ran while one was open for 1% -> 1% of each run, Pallas kernels for 0% -> 0%
where the time goes in v1:
time: 2320 us; the launch traced here: 2290 us
  local copies, waits for them, and re-layouts  1000 us (43%)
  waiting for transfers between devices  665 us (29%)
  other arithmetic  379 us (16%)
  blocking collectives  153 us (7%)
  matrix products  65.3 us (3%)
    pad x192, local copies, waits for them, and re-layouts, block_states(): lax.associative_scan(pair_combine, (factor, source), axis=0)  811 us
    psum x1, waiting for transfers between devices, shards(): lax.psum(lax.psum((gain_grad, in_grad, tap_grads, conv_bias_grad, x_proj_...  401 us
    psum x1, waiting for transfers between devices, shards(): lax.psum((gain_grad, in_grad, tap_grads, conv_bias_grad, x_proj_grad, ste...  263 us
    add x96, other arithmetic, pair_combine(): return (first[0] * second[0], first[1] * second[0] + second[1])  105 us
    all_gather x3, blocking collectives, prefix(): pieces = jax.tree.map(lambda part: lax.all_gather(part, axis), value)  99.6 us
    add x96, other arithmetic, block_states(): lax.associative_scan(pair_combine, (factor, source), axis=0)  87.8 us
    dot_general x12, matrix products, matmul(): jnp.dot(left, right, precision=MATMUL_ACCURACY, preferred_element_type=jn...  65.3 us
    slice x84, local copies, waits for them, and re-layouts, block_states(): lax.associative_scan(pair_combine, (factor, source), axis=0)  54.2 us
  transfers between devices with their start and end apart: 4, of which 3 were waited for; matrix products, arithmetic and copies ran while one was open for 1% of the time, Pallas kernels for 0%

profile of v1, /device:TPU:0, one launch (start us, length us, event | category | flops | bytes accessed | tf_op | source)
XLA Modules:
  0.0 2293.6 jit_solution(2735229972882037936)
XLA Ops:
  9.0 7.8 fusion.71
  23.4 10.3 multiply_reduce_fusion.8
  37.9 33.2 %all-gather.3 = f32[8,1,1536]{2,1,0:T(1,128)S(1)} all-gather(f32[1,1,1536]{2,1,0:T(1,128)S(1)} %reshape.758), channel_id=2, replica_groups=mesh['seq'=8,'batch'=4] {'seq'}, dimensions={0}, use_global_device_ids=true | all-gather | bytes 55296 | tf_op jit(solution)/shard_map/all_gather | solution.py:20
  75.0 414.5 %while.93 = (s32[]{:T(128)}, f32[1,16,1536]{2,1,0:T(8,128)}, f32[4,32,1,1536]{3,2,1,0:T(1,128)}, f32[4,1,16,1536]{3,2,1,0:T(8,128)}, f32[4,32,1,3104]{3,2,1,0:T(...) while((s32[]{:T(128)}, f32[1,16,1536]{2,1,0:T(8,128)}, f32[4,32,1,1536]{3,2,1,0:T(1,128)}, ...), condition=%wide.region_3.4_spmd, body=%wide.region_1.3_spmd.sunk | while | flops 14721026 | bytes 223114064 | solution.py:139
  134.8 10.9 pad.889
  145.8 6.8 pad.887
  152.6 10.9 pad.890
  163.6 6.8 pad.888
  238.4 10.9 pad.889
  249.4 6.8 pad.887
  256.2 10.9 pad.890
  267.2 6.8 pad.888
  342.1 10.9 pad.889
  353.0 6.8 pad.887
  359.9 10.9 pad.890
  370.8 6.8 pad.888
  445.7 10.9 pad.889
  456.6 6.8 pad.887
  463.5 10.9 pad.890
  474.4 6.8 pad.888
  489.5 10.9 while.96
  500.4 32.3 %all-gather.2 = f32[8,16,1536]{2,1,0:T(8,128)S(1)} all-gather(f32[1,16,1536]{2,1,0:T(8,128)} %get-tuple-element.564), channel_id=4, replica_groups=mesh['seq'=8,'batch'=4] {'seq'}, dimensions={0}, use_global_device_ids=true | all-gather | bytes 884736 | tf_op jit(solution)/shard_map/all_gather | solution.py:20
  533.7 11.9 while.97
  545.6 34.0 %all-gather.1 = f32[8,16,1536]{2,1,0:T(8,128)} all-gather(f32[1,16,1536]{2,1,0:T(8,128)} %get-tuple-element.561), channel_id=3, replica_groups=mesh['seq'=8,'batch'=4] {'seq'}, dimensions={0}, use_global_device_ids=true | all-gather | bytes 884736 | tf_op jit(solution)/shard_map/all_gather | solution.py:20
  579.7 11.9 while.95
  591.6 12.4 while.94
  607.1 883.1 %while.98 = (s32[]{:T(128)}, f32[1,16,1536]{2,1,0:T(8,128)S(1)}, f32[16,1536]{1,0:T(8,128)}, f32[4,32,1,3104]{3,1,2,0:T(8,128)}, f32[4,32,1,3104]{3,2,1,0:T(1,12...) while((s32[]{:T(128)}, f32[1,16,1536]{2,1,0:T(8,128)S(1)}, ...), condition=%wide.region_23.24_spmd.clone, body=%wide.region_17.23_spmd.clone.sunk | while | flops 36273152 | bytes 493608896 | solution.py:201
  675.4 10.9 pad.945
  686.3 6.8 pad.943
  693.1 10.9 pad.946
  704.1 7.0 pad.944
  778.5 10.9 pad.961
  789.4 6.8 pad.959
  796.2 11.1 pad.962
  807.3 6.8 pad.960
  896.0 10.9 pad.945
  906.9 6.8 pad.943
  913.8 10.9 pad.946
  924.7 7.0 pad.944
  999.1 10.9 pad.961
  1010.0 6.8 pad.959
  1016.9 11.1 pad.962
  1027.9 6.8 pad.960
  1116.6 10.9 pad.945
  1127.6 6.8 pad.943
  1134.4 10.9 pad.946
  1145.3 7.0 pad.944
  1219.7 10.9 pad.961
  1237.5 11.1 pad.962
  1248.6 6.8 pad.960
  1337.3 10.9 pad.945
  1355.1 10.9 pad.946
  1366.0 7.0 pad.944
  1440.4 10.9 pad.961
  1458.2 11.1 pad.962
  1469.2 6.8 pad.960
  1514.8 7.3 fusion.58
  1526.2 11.3 fusion.44
  1537.6 262.6 %all-reduce.72.cloned.1.call-done = (f32[768,3072]{1,0:T(8,128)}, f32[1536,80]{0,1:T(8,128)}, f32[48,1536]{1,0:T(8,128)}, f32[1536,16]{0,1:T(8,128)}, f32[1536,768]{1,0:T(8,128)}) async-done(((f32[768,3072]{1,0:T(8,128)}, f32[1536,80]{0,1:T(8,128)}, f32[48,1536]{1,0:T(8,128)}, f32[1536,16]{0,1:T(8,128)}, f32[1536,768]{1,0:T(8,128)}), (f32[768,3072]{1,0:T(8,128)}, f32[1536,80]{0,1:T(8,128)}, ...) | async-done | bytes 15040528 | tf_op jit(solution)/shard_map/psum | solution.py:238
  1806.5 12.0 fusion.69
  1818.6 11.5 all-reduce.65
  1830.1 41.8 %all-reduce.63 = (f32[768]{0:T(1024)}, f32[4,1536]{1,0:T(4,128)}, f32[1536]{0:T(1024)}, f32[1536]{0:T(1024)}, f32[1536]{0:T(1024)}) all-reduce(f32[768]{0:T(1024)S(1)} %get-tuple-element.901, f32[4,1536]{1,0:T(4,128)S(1)} %get-tuple-element.902, f32[1536]{0:T(1024)S(1)} %get-tuple-element.903, ...), channel_id=1, replica_groups=mesh['seq'=8,'batch'=4] {'seq'}, use_global_device_ids=true, to_apply=%region_27.28 | all-reduce | flops 11520 | bytes 92160 | tf_op jit(solution)/shard_map/psum | solution.py:237
  1872.8 400.6 %all-reduce.70.cloned.1.call-done = (f32[768,3072]{1,0:T(8,128)}, f32[1536,80]{0,1:T(8,128)}, f32[48,1536]{1,0:T(8,128)}, f32[1536,16]{0,1:T(8,128)}, f32[1536,768]{1,0:T(8,128)}) async-done(((f32[768,3072]{1,0:T(8,128)}, f32[1536,80]{0,1:T(8,128)}, f32[48,1536]{1,0:T(8,128)}, f32[1536,16]{0,1:T(8,128)}, f32[1536,768]{1,0:T(8,128)}), (f32[768,3072]{1,0:T(8,128)}, f32[1536,80]{0,1:T(8,128)}, ...) | async-done | bytes 15040528 | tf_op jit(solution)/shard_map/psum | solution.py:237
  2273.5 8.8 copy.201
  (1581 shorter events, 992.5 us)
Async XLA Ops:
  7.2 26.6 %copy-start = (f32[1536,80]{0,1:T(8,128)S(1)}, f32[1536,80]{0,1:T(8,128)}, u32[]{:S(2)}) copy-start(f32[1536,80]{0,1:T(8,128)} %param.40) | copy-start | bytes 1474564
  7.2 1793.0 %all-reduce.72.cloned.1.call-start = ((), (), s32[]{:S(2)}) async-start(), calls=%async_computation.1 | async-start | bytes 30081024 | tf_op jit(solution)/shard_map/psum | solution.py:238
  9.0 7.8 copy-start.125
  16.8 16.9 copy-start.60
  16.9 6.5 collective-permute-start
  22.1 11.6 copy-start.114
  22.1 11.6 copy-start.116
  22.1 11.6 copy-start.118
  22.1 11.6 copy-start.120
  23.4 10.3 copy-start.122
  23.4 11.4 copy-start.132
  33.7 38.0 %copy-start.63 = (f32[128,1536]{1,0:T(8,128)}, f32[128,1536]{1,0:T(8,128)S(1)}, u32[]{:S(2)}) copy-start(f32[128,1536]{1,0:T(8,128)S(1)} %get-tuple-element.917) | copy-start | bytes 2359300
  152.6 10.9 copy-start.29
  170.4 8.2 copy-start.52
  256.2 10.9 copy-start.29
  274.0 8.3 copy-start.52
  359.9 10.9 copy-start.29
  377.6 8.2 copy-start.52
  463.5 10.9 copy-start.29
  481.3 8.2 copy-start.52
  500.4 33.3 %copy-start.69 = (f32[1,16,1536]{2,1,0:T(8,128)S(1)}, f32[1,16,1536]{2,1,0:T(8,128)}, u32[]{:S(2)}) copy-start(f32[1,16,1536]{2,1,0:T(8,128)} %custom-call.2) | copy-start | bytes 294916
  533.7 46.0 %copy-start.87 = (f32[1,16,1536]{2,1,0:T(8,128)S(1)}, f32[1,16,1536]{2,1,0:T(8,128)}, u32[]{:S(2)}) copy-start(f32[1,16,1536]{2,1,0:T(8,128)} %custom-call) | copy-start | bytes 294916
  607.3 7.7 copy-start.36
  693.1 10.9 copy-start.31
  704.1 7.0 copy-start.71
  711.1 7.0 copy-start.57
  796.2 11.1 copy-start.30
  807.3 6.9 copy-start.56
  807.3 6.9 copy-start.68
  827.9 7.7 copy-start.36
  913.8 10.9 copy-start.31
  924.7 7.0 copy-start.71
  931.7 7.0 copy-start.57
  1016.9 11.1 copy-start.30
  1027.9 6.9 copy-start.56
  1027.9 6.9 copy-start.68
  1048.5 7.7 copy-start.36
  1134.4 10.9 copy-start.31
  1145.3 7.0 copy-start.71
  1152.4 7.0 copy-start.57
  1237.5 11.1 copy-start.30
  1248.6 6.9 copy-start.56
  1248.6 6.9 copy-start.68
  1269.2 7.7 copy-start.36
  1355.1 10.9 copy-start.31
  1366.0 7.0 copy-start.71
  1373.0 7.0 copy-start.57
  1458.2 11.1 copy-start.30
  1469.2 6.9 copy-start.56
  1469.2 6.9 copy-start.68
  1507.4 7.4 copy-start.101
  1513.5 11.1 collective-permute-start.1
  1514.8 7.4 copy-start.90
  1514.8 7.4 copy-start.99
  1514.8 7.4 copy-start.115
  1514.8 7.4 copy-start.123
  1537.5 735.9 %all-reduce.70.cloned.1.call-start = ((), (), s32[]{:S(2)}) async-start(), calls=%async_computation | async-start | bytes 30081024 | tf_op jit(solution)/shard_map/psum | solution.py:237
  1806.5 12.1 copy-start.129
  1806.5 65.4 %copy-start.102 = (f32[1,128,768]{2,1,0:T(8,128)S(1)}, f32[1,128,768]{2,1,0:T(8,128)}, u32[]{:S(2)}) copy-start(f32[1,128,768]{2,1,0:T(8,128)} %param.47) | copy-start | bytes 1179652
  1806.5 65.4 %copy-start.130 = (f32[128]{0:T(128)S(1)}, f32[128]{0:T(128)}, u32[]{:S(2)}) copy-start(f32[128]{0:T(128)} %get-tuple-element.1015) | copy-start | bytes 1540
  2273.5 10.9 slice-start.1
  2273.5 8.8 copy-start.105
  2273.5 9.5 copy-start.108
  2273.5 10.9 slice-start.2
  (325 other events, 780.4 us)
Sparse Core Ops, SparseCore 0:
  1537.7 262.5 all-reduce.71
  1806.4 467.0 all-reduce.69
